TPU v7x, 32 devices: a whole 2x2x4 slice. The times are simulated.
32 devices in a mesh: depth: 16 (over z, y, x), rows: 2 (over core).
Axes of the slice: x: 2, y: 2, z: 4, core: 2. Of those that a mesh axis runs over, the one named last changes fastest.
Arguments:
- field: bfloat16 [256, 128, 1024], P('depth', 'rows'), may hold values from -6 to 6
- tf_centers: float32 [4], replicated, may hold values from -1.5 to 1.5
- tf_widths: float32 [4], replicated, may hold values from 0.4 to 1.2
- tf_density: float32 [4], replicated, may hold values from 0.5 to 4
- tf_colors: float32 [3, 4], replicated, may hold values from 0.1 to 1
- light: float32 [3], replicated, may hold values from 0.5 to 1.5
Outputs:
- image: float32 [4, 128, 1024], P(None, 'rows', 'depth')
All inputs are finite; a program needn't handle non-finite values.
Results may differ from a plain program's by a relative error of at most 0.0003.
Values may be sent and summed in bfloat16 or wider, within the bound.
A program may use at most 64 MiB of HBM per device.

v0:
```python
import functools
import math

import jax
import jax.numpy as jnp
from jax import lax
from jax.experimental import pallas as pl
from jax.experimental.pallas import tpu as pltpu
from jax.sharding import PartitionSpec as P

MESH = pl.DeviceIdType.MESH
LANES = 128
SUB = 8
LAG = 10
EARLY = 16
READY = 0
LOG2E = math.log2(math.e)


def kernel(
    n, m, field, *rest,
):
    sources, image, tables = rest[:5], rest[5], rest[6:11]
    centers, widths, density, colors, light = tables
    (
        brick, halo_z, halo_y, cells, partial, packed, arrived, joined, kept, parts,
        table_sem, brick_sem, z_send, z_recv, y_send, y_recv, pair_send, pair_recv, own_send, own_recv,
    ) = rest[11:]
    planes, rows, columns = field.shape
    tiles = columns // LANES
    k = LANES * n // columns
    band_rows = SUB * k
    bands = rows // band_rows
    units = bands * tiles
    half = k // 2
    me = lax.axis_index("depth")
    row = lax.axis_index("rows")
    parity = lax.rem(me, 2)
    group = me // 2
    partner = me + 1 - 2 * parity
    last = n - 1

    barrier = pltpu.get_barrier_semaphore()

    def signal(where):
        pl.semaphore_signal(barrier, inc=1, device_id=where, device_id_type=MESH)

    load = pltpu.make_async_copy(field, brick, brick_sem)
    load.start()
    table_loads = [
        pltpu.make_async_copy(source, table, table_sem.at[i])
        for i, (source, table) in enumerate(zip(sources, tables))
    ]
    for copy in table_loads:
        copy.start()

    @pl.when(me > 0)
    def _():
        signal({"depth": me - 1})

    @pl.when(me < last)
    def _():
        signal({"depth": me + 1})

    @pl.when(row > 0)
    def _():
        signal({"rows": row - 1})

    @pl.when(row < m - 1)
    def _():
        signal({"rows": row + 1})

    signal({"depth": partner})
    for step in range(1, n // 2):
        signal({"depth": lax.rem(group + step, n // 2) * 2 + parity})

    for copy in table_loads:
        copy.wait()
    load.wait()

    zero_row = jnp.zeros((cells.shape[2], LANES), jnp.float32)

    def widen(z, carry):
        for t in range(tiles):
            cells[z, 1 + t, SUB : SUB + rows, :] = brick[
                z, :, t * LANES : (t + 1) * LANES
            ].astype(jnp.float32)
        cells[z, 0] = zero_row
        cells[z, tiles + 1] = zero_row
        return carry

    lax.fori_loop(0, planes, widen, 0)

    def band_of(i):
        return lax.rem(i + 1, bands)

    def z_copy(b, side):
        span = pl.ds(pl.multiple_of(b * band_rows, band_rows), band_rows)
        source = planes - 1 if side == 0 else 0
        where = me + 1 if side == 0 else me - 1
        return pltpu.make_async_remote_copy(
            src_ref=field.at[source, span],
            dst_ref=halo_z.at[side, span],
            send_sem=z_send.at[side],
            recv_sem=z_recv.at[side, b],
            device_id={"depth": where},
            device_id_type=MESH,
        )

    def y_copy(side):
        start = rows - SUB if side == 0 else 0
        where = row + 1 if side == 0 else row - 1
        return pltpu.make_async_remote_copy(
            src_ref=field.at[:, pl.ds(start, SUB)],
            dst_ref=halo_y.at[side],
            send_sem=y_send.at[side],
            recv_sem=y_recv.at[side],
            device_id={"rows": where},
            device_id_type=MESH,
        )

    has_source = (me > 0, me < last)
    has_target = (me < last, me > 0)
    row_source = (row > 0, row < m - 1)
    row_target = (row < m - 1, row > 0)

    for side in range(2):
        @pl.when(jnp.logical_not(has_source[side]))
        def _(side=side):
            halo_z[side] = jnp.zeros(halo_z.shape[1:], halo_z.dtype)

    def start_halos():
        expected = (
            (me > 0).astype(jnp.int32) + (me < last).astype(jnp.int32)
            + (row > 0).astype(jnp.int32) + (row < m - 1).astype(jnp.int32)
            + n // 2
        )
        pl.semaphore_wait(barrier, expected)
        for side in range(2):
            @pl.when(has_target[side])
            def _(side=side):
                def send(i, carry):
                    z_copy(band_of(i), side).start()
                    return carry

                lax.fori_loop(0, bands, send, 0)

        for side in range(2):
            @pl.when(row_target[side])
            def _(side=side):
                y_copy(side).start()

    def full(value):
        return jnp.full((SUB, LANES), value, jnp.float32)

    bumps = centers.shape[0]
    centre = [centers[i] for i in range(bumps)]
    narrow = []
    dense = []
    step_size = 0.5 / (planes * n)
    for i in range(bumps):
        w = full(widths[i])
        narrow.append((-LOG2E / (w * w))[:1])
        dense.append(density[i] * (-LOG2E * step_size * 4.0))
    ray = [full(light[i]) for i in range(3)]
    scale = 0.7 / jnp.sqrt(ray[0] * ray[0] + ray[1] * ray[1] + ray[2] * ray[2])
    ray = [(r * scale)[:1] for r in ray]
    lane = lax.broadcasted_iota(jnp.int32, (band_rows, LANES), 1)
    first_lane = lane == 0
    last_lane = lane == LANES - 1
    small = lax.broadcasted_iota(jnp.int32, (SUB, LANES), 1)

    def bump_sum(weights, values):
        total = weights[0] * values[0]
        for w, v in zip(weights[1:], values[1:]):
            total = total + w * v
        return total

    def place(s):
        b = band_of(s // tiles)
        t = lax.rem(lax.rem(s, tiles) + 1 + me // k, tiles)
        return b, t

    def pair_copy(s):
        return pltpu.make_async_remote_copy(
            src_ref=packed.at[s, 1 - parity],
            dst_ref=arrived.at[s],
            send_sem=pair_send,
            recv_sem=pair_recv.at[s],
            device_id={"depth": partner},
            device_id_type=MESH,
        )

    def own_copy(s, i):
        b, t = place(s)
        return pltpu.make_async_remote_copy(
            src_ref=joined.at[s, i],
            dst_ref=parts.at[group, b],
            send_sem=own_send,
            recv_sem=own_recv,
            device_id={"depth": t * k + 2 * i + parity},
            device_id_type=MESH,
        )

    def wait_halos(s):
        b, t = place(s)

        @pl.when(lax.rem(s, tiles) == 0)
        def _():
            for side in range(2):
                @pl.when(has_source[side])
                def _(side=side):
                    z_copy(b, side).wait_recv()

        @pl.when(s == max(bands - 2, 0) * tiles)
        def _():
            for side in range(2):
                spot = 0 if side == 0 else SUB + rows

                @pl.when(row_source[side])
                def _(side=side, spot=spot):
                    y_copy(side).wait_recv()

                    def put(z, carry):
                        for t in range(tiles):
                            cells[z, 1 + t, spot : spot + SUB, :] = halo_y[
                                side, z, :, t * LANES : (t + 1) * LANES
                            ].astype(jnp.float32)
                        return carry

                    lax.fori_loop(0, planes, put, 0)

                @pl.when(jnp.logical_not(row_source[side]))
                def _(spot=spot):
                    def put(z, carry):
                        for t in range(tiles):
                            cells[z, 1 + t, spot : spot + SUB, :] = jnp.zeros(
                                (SUB, LANES), jnp.float32
                            )
                        return carry

                    lax.fori_loop(0, planes, put, 0)

    def shade(s, first, last):
        b, t = place(s)
        base = pl.multiple_of(b * band_rows, band_rows)
        span = pl.ds(base + SUB, band_rows)
        halo_span = pl.ds(base, band_rows)
        halo_columns = pl.ds(pl.multiple_of(t * LANES, LANES), LANES)
        if first:
            through = jnp.ones((band_rows, LANES), jnp.float32)
            depth = jnp.zeros((band_rows, LANES), jnp.float32)
            sums = [jnp.zeros((band_rows, LANES), jnp.float32) for _ in range(bumps)]
        else:
            through, depth, *sums = [partial[s, i] for i in range(bumps + 2)]
        order = list(range(1, planes - 1)) if first else []
        for z in order + ([planes - 1, 0] if last else []):
            v = cells[z, 1 + t, span, :]
            if z == 0:
                before = halo_z[0, halo_span, halo_columns].astype(jnp.float32)
            else:
                before = cells[z - 1, 1 + t, span, :]
            if z == planes - 1:
                after = halo_z[1, halo_span, halo_columns].astype(jnp.float32)
            else:
                after = cells[z + 1, 1 + t, span, :]
            dz = after - before
            dy = (
                cells[z, 1 + t, pl.ds(base + SUB + 1, band_rows), :]
                - cells[z, 1 + t, pl.ds(base + SUB - 1, band_rows), :]
            )
            left = jnp.where(
                first_lane,
                pltpu.roll(cells[z, t, span, :], 1, 1),
                pltpu.roll(v, 1, 1),
            )
            right = jnp.where(
                last_lane,
                pltpu.roll(cells[z, 2 + t, span, :], LANES - 1, 1),
                pltpu.roll(v, LANES - 1, 1),
            )
            dx = right - left
            r = lax.rsqrt(dz * dz + dy * dy + (dx * dx + 4.0))
            facing = jnp.abs(dz * ray[0] + dy * ray[1] + dx * ray[2])
            lighting = 0.3 + facing * r
            bump = []
            for i in range(bumps):
                u = v - centre[i]
                bump.append(jnp.exp2((u * u) * narrow[i]))
            tau = bump_sum(dense, bump) * (0.3125 - r * r)
            depth = depth + tau
            seen = jnp.exp2(tau)
            front = jnp.ones_like(seen) if z == 0 else through
            rest = front * seen
            inverse = lax.rsqrt((bump[0] + bump[1]) + (sum(bump[3:], bump[2]) + 0.1))
            weight = (front - rest) * lighting * (inverse * inverse)
            if z == 0:
                sums = [seen * total for total in sums]
            else:
                through = rest
            sums = [total + weight * value for total, value in zip(sums, bump)]
        if not last:
            for i, value in enumerate([through, depth] + sums):
                partial[s, i] = value
            return
        channels = [
            bump_sum([colors[c, i] for i in range(bumps)], sums) for c in range(3)
        ] + [depth]
        for c in range(4):
            blocks = [channels[c][i * SUB : (i + 1) * SUB] for i in range(k)]
            for h in range(k):
                out = None
                for i in range(k):
                    shift = ((i - h) * LANES // k) % LANES
                    piece = pltpu.roll(blocks[i], shift, 1) if shift else blocks[i]
                    out = piece if i == 0 else jnp.where(small >= i * LANES // k, piece, out)
                packed[s, h % 2, h // 2, c] = out
        pair_copy(s).start()

    def combine(s):
        b, t = place(s)
        pair_copy(s).wait_recv()
        for i in range(half):
            mine = [packed[s, parity, i, c] for c in range(4)]
            other = [arrived[s, i, c] for c in range(4)]
            front = parity == 0
            mine_scale = jnp.where(front, 1.0, jnp.exp2(other[3]))
            other_scale = jnp.where(front, jnp.exp2(mine[3]), 1.0)
            both = [
                mine[c] * mine_scale + other[c] * other_scale for c in range(3)
            ] + [mine[3] + other[3]]
            for c in range(4):
                kept[b, i, c] = both[c]
                joined[s, i, c] = both[c]

            @pl.when(t * k + 2 * i + parity != me)
            def _():
                own_copy(s, i).start()

    lag = min(LAG, units)
    early = min(EARLY, tiles * max(bands - 2, 0))
    ready = min(READY, early)

    def inner(s, carry):
        shade(s, True, False)
        return carry

    def outer(s, carry):
        @pl.when(jnp.logical_and(lax.rem(s, tiles) == 0, s > 0))
        def _():
            wait_halos(s)

        shade(s, False, True)

        @pl.when(s >= lag)
        def _():
            combine(s - lag)

        return carry

    def step(s, carry):
        @pl.when(jnp.logical_and(lax.rem(s, tiles) == 0, s > 0))
        def _():
            wait_halos(s)

        shade(s, True, True)

        @pl.when(s >= lag)
        def _():
            combine(s - lag)

        return carry

    lax.fori_loop(0, ready, inner, 0)
    start_halos()
    lax.fori_loop(ready, early, inner, 0)
    wait_halos(0)
    lax.fori_loop(0, early, outer, 0)
    lax.fori_loop(early, units, step, 0)

    def drain(s, carry):
        combine(s)
        return carry

    lax.fori_loop(units - lag, units, drain, 0)

    everything = parts.at[pl.ds(0, n // 2 - 1)]
    all_parts = pltpu.make_async_remote_copy(
        src_ref=everything,
        dst_ref=everything,
        send_sem=own_send,
        recv_sem=own_recv,
        device_id={"depth": partner},
        device_id_type=MESH,
    )
    all_parts.wait_recv()
    for b in range(bands):
        parts[group, b] = kept[b, lax.rem(me, k) // 2]

    for b in range(bands):
        depth = jnp.zeros((SUB, LANES), jnp.float32)
        tint = [jnp.zeros((SUB, LANES), jnp.float32) for _ in range(3)]
        for q in range(n // 2):
            seen = jnp.exp2(depth)
            tint = [tint[c] + seen * parts[q, b, c] for c in range(3)]
            depth = depth + parts[q, b, 3]
        result = tint + [1.0 - jnp.exp2(depth)]
        for c in range(4):
            for i in range(k):
                shift = (-i * LANES // k) % LANES
                piece = pltpu.roll(result[c], shift, 1) if shift else result[c]
                start = b * band_rows + i * SUB
                image[c, start : start + SUB, :] = piece[:, : LANES // k]

    for side in range(2):
        @pl.when(has_target[side])
        def _(side=side):
            pltpu.make_async_remote_copy(
                src_ref=field.at[0],
                dst_ref=halo_z.at[side],
                send_sem=z_send.at[side],
                recv_sem=z_recv.at[side, 0],
                device_id={"depth": partner},
                device_id_type=MESH,
            ).wait_send()

        @pl.when(row_target[side])
        def _(side=side):
            y_copy(side).wait_send()

    pltpu.make_async_remote_copy(
        src_ref=arrived,
        dst_ref=arrived,
        send_sem=pair_send,
        recv_sem=pair_recv.at[0],
        device_id={"depth": partner},
        device_id_type=MESH,
    ).wait_send()
    all_parts.wait_send()


def solution(mesh):
    n, m = mesh.shape["depth"], mesh.shape["rows"]

    def shards(field, centers, widths, density, colors, light):
        planes, rows, columns = field.shape
        tiles = columns // LANES
        k = LANES * n // columns
        bands = rows // (SUB * k)
        units = bands * tiles
        half = k // 2
        block = (4, SUB, LANES)
        vmem, dma = pltpu.VMEM, pltpu.SemaphoreType.DMA
        operands = (field, centers, widths, density, colors, light)
        return pl.pallas_call(
            functools.partial(kernel, n, m),
            out_shape=jax.ShapeDtypeStruct((4, rows, columns // n), jnp.float32),
            in_specs=[pl.BlockSpec(memory_space=pltpu.HBM)] * 6,
            out_specs=pl.BlockSpec(memory_space=pltpu.VMEM),
            scratch_shapes=[pltpu.SMEM(a.shape, a.dtype) for a in operands[1:]]
            + [
                vmem(field.shape, field.dtype),
                vmem((2, rows, columns), field.dtype),
                vmem((2, planes, SUB, columns), field.dtype),
                vmem((planes, tiles + 2, rows + 2 * SUB, LANES), jnp.float32),
                vmem(
                    (EARLY, centers.shape[0] + 2, SUB * k, LANES), jnp.float32
                ),
                vmem((units, 2, half) + block, jnp.float32),
                vmem((units, half) + block, jnp.float32),
                vmem((units, half) + block, jnp.float32),
                vmem((bands, half) + block, jnp.float32),
                vmem((n // 2, bands) + block, jnp.float32),
                dma((5,)),
                dma,
                dma((2,)),
                dma((2, bands)),
                dma((2,)),
                dma((2,)),
                dma,
                dma((units,)),
                dma,
                dma,
            ],
            compiler_params=pltpu.CompilerParams(
                collective_id=0, has_side_effects=True, vmem_limit_bytes=67043328
            ),
            name="raycast",
        )(*operands)

    placed = (P("depth", "rows", None), P(), P(), P(), P(), P())
    return jax.shard_map(
        shards, mesh=mesh, in_specs=placed, out_specs=P(None, "rows", "depth"), check_vma=False
    )
```

profile of v0, /device:TPU:0, one launch (start us, length us, event | category | flops | bytes accessed | tf_op | source)
XLA Modules:
  0.0 31.8 jit_solution(10190601627435418122)
XLA Ops:
  0.0 30.2 %raycast.1 = f32[4,64,64]{2,1,0:T(8,128)} custom-call(bf16[16,64,1024]{2,1,0:T(8,128)(2,1)} %field.1, f32[4]{0:T(128)} %rest_0_.1, f32[4]{0:T(128)} %rest_1_.1, f32[4]{0:T(128)} %rest_2_.1, f32[3,4]{1,0:T(4,128)} %rest_3_.1, f32[3]{0:T(128)} %rest_4_.1), custom_call_target="tpu_custom_call" | custom-call | tf_op jit(solution)/shard_map/raycast/pallas_call | solution.py:455
  30.2 1.6 %copy.8 = f32[4,64,64]{2,1,0:T(8,128)} copy(f32[4,64,64]{2,1,0:T(8,128)} %raycast.1) | data formatting | bytes 131072
where the time goes:
time: 31.9 us; the launch traced here: 31.8 us
  Pallas kernels  30.2 us (95%)
  local copies, waits for them, and re-layouts  1.57 us (5%)
    pallas_call x1, Pallas kernels, shards(): pl.pallas_call(functools.partial(kernel, n, m), out_shape=jax.ShapeDtypeS...  30.2 us
    unnamed x1, local copies, waits for them, and re-layouts  1.57 us

commit v1 on v0

--- a/solution.py
+++ b/solution.py
@@ -11,10 +11,29 @@
 MESH = pl.DeviceIdType.MESH
 LANES = 128
 SUB = 8
-LAG = 10
+LAG = 8
+WIDE = 2
+DRAIN = 2
 EARLY = 16
-READY = 0
 LOG2E = math.log2(math.e)
+POWER = 8
+RANGE = 11.0
+DITHER = LOG2E / 1024 / POWER
+
+
+def offset_of(group):
+    return RANGE + group * DITHER
+
+
+def encode(x, scale):
+    y = x * scale
+    for _ in range(POWER.bit_length() - 1):
+        y = y * y
+    return y
+
+
+def decode(y, offset):
+    return jnp.exp2(jnp.log2(y) * (1 / POWER) - offset)
 
 
 def kernel(
@@ -23,7 +42,7 @@
     sources, image, tables = rest[:5], rest[5], rest[6:11]
     centers, widths, density, colors, light = tables
     (
-        brick, halo_z, halo_y, cells, partial, packed, arrived, joined, kept, parts,
+        brick, halo_z, halo_y, cells, fixed, partial, held, packed, arrived, joined, kept, parts,
         table_sem, brick_sem, z_send, z_recv, y_send, y_recv, pair_send, pair_recv, own_send, own_recv,
     ) = rest[11:]
     planes, rows, columns = field.shape
@@ -154,20 +173,22 @@
         return jnp.full((SUB, LANES), value, jnp.float32)
 
     bumps = centers.shape[0]
-    centre = [centers[i] for i in range(bumps)]
-    narrow = []
-    dense = []
     step_size = 0.5 / (planes * n)
     for i in range(bumps):
         w = full(widths[i])
-        narrow.append((-LOG2E / (w * w))[:1])
-        dense.append(density[i] * (-LOG2E * step_size * 4.0))
-    ray = [full(light[i]) for i in range(3)]
-    scale = 0.7 / jnp.sqrt(ray[0] * ray[0] + ray[1] * ray[1] + ray[2] * ray[2])
-    ray = [(r * scale)[:1] for r in ray]
-    lane = lax.broadcasted_iota(jnp.int32, (band_rows, LANES), 1)
+        fixed[i] = full(centers[i])
+        fixed[bumps + i] = -LOG2E / (w * w)
+        fixed[2 * bumps + i] = full(density[i] * (-LOG2E * step_size * 4.0))
+    axes = [full(light[i]) for i in range(3)]
+    scale = 0.7 / jnp.sqrt(axes[0] * axes[0] + axes[1] * axes[1] + axes[2] * axes[2])
+    for i in range(3):
+        fixed[3 * bumps + i] = axes[i] * scale
+    lane = lax.broadcasted_iota(jnp.int32, (SUB, LANES), 1)
     first_lane = lane == 0
     last_lane = lane == LANES - 1
+    cell_shape = (k, SUB, LANES)
+    offset = full(offset_of(group.astype(jnp.float32)))[:1]
+    scale_up = jnp.exp2(offset)
     small = lax.broadcasted_iota(jnp.int32, (SUB, LANES), 1)
 
     def bump_sum(weights, values):
@@ -248,36 +269,48 @@
         halo_span = pl.ds(base, band_rows)
         halo_columns = pl.ds(pl.multiple_of(t * LANES, LANES), LANES)
         if first:
-            through = jnp.ones((band_rows, LANES), jnp.float32)
-            depth = jnp.zeros((band_rows, LANES), jnp.float32)
-            sums = [jnp.zeros((band_rows, LANES), jnp.float32) for _ in range(bumps)]
+            through = jnp.ones(cell_shape, jnp.float32)
+            depth = jnp.zeros(cell_shape, jnp.float32)
+            sums = [jnp.zeros(cell_shape, jnp.float32) for _ in range(bumps)]
         else:
             through, depth, *sums = [partial[s, i] for i in range(bumps + 2)]
+        centre = [fixed[i] for i in range(bumps)]
+        narrow = [fixed[bumps + i] for i in range(bumps)]
+        dense = [fixed[2 * bumps + i] for i in range(bumps)]
+        ray = [fixed[3 * bumps + i] for i in range(3)]
+
+        def cell(z, tile, rows):
+            return cells[z, tile, rows, :].reshape(cell_shape)
+
+        def edge(side):
+            values = halo_z[side, halo_span, halo_columns].astype(jnp.float32)
+            return values.reshape(cell_shape)
+
         order = list(range(1, planes - 1)) if first else []
         for z in order + ([planes - 1, 0] if last else []):
-            v = cells[z, 1 + t, span, :]
+            v = cell(z, 1 + t, span)
             if z == 0:
-                before = halo_z[0, halo_span, halo_columns].astype(jnp.float32)
+                before = edge(0)
             else:
-                before = cells[z - 1, 1 + t, span, :]
+                before = cell(z - 1, 1 + t, span)
             if z == planes - 1:
-                after = halo_z[1, halo_span, halo_columns].astype(jnp.float32)
+                after = edge(1)
             else:
-                after = cells[z + 1, 1 + t, span, :]
+                after = cell(z + 1, 1 + t, span)
             dz = after - before
             dy = (
-                cells[z, 1 + t, pl.ds(base + SUB + 1, band_rows), :]
-                - cells[z, 1 + t, pl.ds(base + SUB - 1, band_rows), :]
+                cell(z, 1 + t, pl.ds(base + SUB + 1, band_rows))
+                - cell(z, 1 + t, pl.ds(base + SUB - 1, band_rows))
             )
             left = jnp.where(
                 first_lane,
-                pltpu.roll(cells[z, t, span, :], 1, 1),
-                pltpu.roll(v, 1, 1),
+                pltpu.roll(cell(z, t, span), 1, 2),
+                pltpu.roll(v, 1, 2),
             )
             right = jnp.where(
                 last_lane,
-                pltpu.roll(cells[z, 2 + t, span, :], LANES - 1, 1),
-                pltpu.roll(v, LANES - 1, 1),
+                pltpu.roll(cell(z, 2 + t, span), LANES - 1, 2),
+                pltpu.roll(v, LANES - 1, 2),
             )
             dx = right - left
             r = lax.rsqrt(dz * dz + dy * dy + (dx * dx + 4.0))
@@ -305,84 +338,118 @@
             return
         channels = [
             bump_sum([colors[c, i] for i in range(bumps)], sums) for c in range(3)
-        ] + [depth]
+        ] + [-depth]
+        codes = [[] for _ in range(k)]
         for c in range(4):
-            blocks = [channels[c][i * SUB : (i + 1) * SUB] for i in range(k)]
+            blocks = [channels[c][i] for i in range(k)]
             for h in range(k):
                 out = None
                 for i in range(k):
                     shift = ((i - h) * LANES // k) % LANES
                     piece = pltpu.roll(blocks[i], shift, 1) if shift else blocks[i]
                     out = piece if i == 0 else jnp.where(small >= i * LANES // k, piece, out)
-                packed[s, h % 2, h // 2, c] = out
-        pair_copy(s).start()
-
-    def combine(s):
+                held[s, h % 2, h // 2, c] = out
+                codes[h].append(encode(out, scale_up))
+        for h in range(k):
+            for pair in range(2):
+                packed[s, h % 2, h // 2, pair] = jnp.concatenate(
+                    codes[h][2 * pair : 2 * pair + 2]
+                ).astype(jnp.bfloat16)
+
+    def merge(s):
         b, t = place(s)
-        pair_copy(s).wait_recv()
         for i in range(half):
-            mine = [packed[s, parity, i, c] for c in range(4)]
-            other = [arrived[s, i, c] for c in range(4)]
+            mine = [held[s, parity, i, c] for c in range(4)]
+            sent = [
+                decode(arrived[s, i, pair].astype(jnp.float32), offset) for pair in range(2)
+            ]
+            other = [sent[c // 2][c % 2 * SUB : (c % 2 + 1) * SUB] for c in range(4)]
             front = parity == 0
-            mine_scale = jnp.where(front, 1.0, jnp.exp2(other[3]))
-            other_scale = jnp.where(front, jnp.exp2(mine[3]), 1.0)
+            mine_scale = jnp.where(front, 1.0, jnp.exp2(-other[3]))
+            other_scale = jnp.where(front, jnp.exp2(-mine[3]), 1.0)
             both = [
                 mine[c] * mine_scale + other[c] * other_scale for c in range(3)
             ] + [mine[3] + other[3]]
-            for c in range(4):
-                kept[b, i, c] = both[c]
-                joined[s, i, c] = both[c]
-
+            for pair in range(2):
+                code = jnp.concatenate(
+                    [encode(both[2 * pair + c], scale_up) for c in range(2)]
+                ).astype(jnp.bfloat16)
+                kept[b, i, pair] = code
+                joined[s, i, pair] = code
+
+    def pass_on(s):
+        b, t = place(s)
+        for i in range(half):
             @pl.when(t * k + 2 * i + parity != me)
-            def _():
+            def _(i=i):
                 own_copy(s, i).start()
 
-    lag = min(LAG, units)
     early = min(EARLY, tiles * max(bands - 2, 0))
-    ready = min(READY, early)
+    early = early - early % (2 * WIDE)
+    late = early // 2 if early else min(LAG, units)
+    turn = early + late
 
     def inner(s, carry):
         shade(s, True, False)
         return carry
 
-    def outer(s, carry):
+    def halos_for(s):
         @pl.when(jnp.logical_and(lax.rem(s, tiles) == 0, s > 0))
         def _():
             wait_halos(s)
 
-        shade(s, False, True)
-
-        @pl.when(s >= lag)
-        def _():
-            combine(s - lag)
-
+    def outer(i, carry):
+        first = i * WIDE
+        for w in range(WIDE):
+            halos_for(first + w)
+        for w in range(WIDE):
+            shade(first + w, False, True)
+        for w in range(WIDE):
+            pair_copy(first + w).start()
         return carry
 
-    def step(s, carry):
-        @pl.when(jnp.logical_and(lax.rem(s, tiles) == 0, s > 0))
-        def _():
-            wait_halos(s)
-
-        shade(s, True, True)
-
-        @pl.when(s >= lag)
-        def _():
-            combine(s - lag)
-
-        return carry
-
-    lax.fori_loop(0, ready, inner, 0)
+    def step_with(merges):
+        def step(s, carry):
+            halos_for(s)
+            ready = merges(s)
+            for u in ready:
+                pair_copy(u).wait_recv()
+            for u in ready:
+                merge(u)
+            shade(s, True, True)
+            pair_copy(s).start()
+            for u in ready:
+                pass_on(u)
+            return carry
+
+        return step
+
+    def drain_from(first, width):
+        def drain(i, carry):
+            ready = [first + i * width + w for w in range(width)]
+            for u in ready:
+                pair_copy(u).wait_recv()
+            for u in ready:
+                merge(u)
+            for u in ready:
+                pass_on(u)
+            return carry
+
+        return drain
+
     start_halos()
-    lax.fori_loop(ready, early, inner, 0)
+    lax.fori_loop(0, early, inner, 0)
     wait_halos(0)
-    lax.fori_loop(0, early, outer, 0)
-    lax.fori_loop(early, units, step, 0)
-
-    def drain(s, carry):
-        combine(s)
-        return carry
-
-    lax.fori_loop(units - lag, units, drain, 0)
+    lax.fori_loop(0, early // WIDE, outer, 0)
+    if early:
+        lax.fori_loop(
+            early, turn, step_with(lambda s: [2 * (s - early), 2 * (s - early) + 1]), 0
+        )
+    else:
+        lax.fori_loop(0, late, step_with(lambda s: []), 0)
+    lax.fori_loop(turn, units, step_with(lambda s: [s - late]), 0)
+    width = DRAIN if late % DRAIN == 0 else 1
+    lax.fori_loop(0, late // width, drain_from(units - late, width), 0)
 
     everything = parts.at[pl.ds(0, n // 2 - 1)]
     all_parts = pltpu.make_async_remote_copy(
@@ -401,10 +468,14 @@
         depth = jnp.zeros((SUB, LANES), jnp.float32)
         tint = [jnp.zeros((SUB, LANES), jnp.float32) for _ in range(3)]
         for q in range(n // 2):
-            seen = jnp.exp2(depth)
-            tint = [tint[c] + seen * parts[q, b, c] for c in range(3)]
-            depth = depth + parts[q, b, 3]
-        result = tint + [1.0 - jnp.exp2(depth)]
+            seen = jnp.exp2(-depth)
+            sent = [
+                decode(parts[q, b, pair].astype(jnp.float32), offset_of(q)) for pair in range(2)
+            ]
+            part = [sent[c // 2][c % 2 * SUB : (c % 2 + 1) * SUB] for c in range(4)]
+            tint = [tint[c] + seen * part[c] for c in range(3)]
+            depth = depth + part[3]
+        result = tint + [1.0 - jnp.exp2(-depth)]
         for c in range(4):
             for i in range(k):
                 shift = (-i * LANES // k) % LANES
@@ -450,6 +521,7 @@
         units = bands * tiles
         half = k // 2
         block = (4, SUB, LANES)
+        code = (2, 2 * SUB, LANES)
         vmem, dma = pltpu.VMEM, pltpu.SemaphoreType.DMA
         operands = (field, centers, widths, density, colors, light)
         return pl.pallas_call(
@@ -463,14 +535,16 @@
                 vmem((2, rows, columns), field.dtype),
                 vmem((2, planes, SUB, columns), field.dtype),
                 vmem((planes, tiles + 2, rows + 2 * SUB, LANES), jnp.float32),
+                vmem((3 * centers.shape[0] + 3, SUB, LANES), jnp.float32),
                 vmem(
-                    (EARLY, centers.shape[0] + 2, SUB * k, LANES), jnp.float32
+                    (EARLY, centers.shape[0] + 2, k, SUB, LANES), jnp.float32
                 ),
                 vmem((units, 2, half) + block, jnp.float32),
-                vmem((units, half) + block, jnp.float32),
-                vmem((units, half) + block, jnp.float32),
-                vmem((bands, half) + block, jnp.float32),
-                vmem((n // 2, bands) + block, jnp.float32),
+                vmem((units, 2, half) + code, jnp.bfloat16),
+                vmem((units, half) + code, jnp.bfloat16),
+                vmem((units, half) + code, jnp.bfloat16),
+                vmem((bands, half) + code, jnp.bfloat16),
+                vmem((n // 2, bands) + code, jnp.bfloat16),
                 dma((5,)),
                 dma,
                 dma((2,)),

time: 31.9 us -> 29.4 us (0.922)
  Pallas kernels: 30.2 us -> 27.7 us
    pallas_call x1, Pallas kernels: 30.2 us -> 27.7 us  [shards(): pl.pallas_call(functools.partial(kernel, n, m), out_shape=jax.ShapeDtypeS...]
where the time goes in v1:
time: 29.4 us; the launch traced here: 29.3 us
  Pallas kernels  27.7 us (94%)
  local copies, waits for them, and re-layouts  1.57 us (5%)
    pallas_call x1, Pallas kernels, shards(): pl.pallas_call(functools.partial(kernel, n, m), out_shape=jax.ShapeDtypeS...  27.7 us
    unnamed x1, local copies, waits for them, and re-layouts  1.57 us

profile of v1, /device:TPU:0, one launch (start us, length us, event | category | flops | bytes accessed | tf_op | source)
XLA Modules:
  0.0 29.3 jit_solution(17865428259803429308)
XLA Ops:
  0.0 27.7 %raycast.1 = f32[4,64,64]{2,1,0:T(8,128)} custom-call(bf16[16,64,1024]{2,1,0:T(8,128)(2,1)} %field.1, f32[4]{0:T(128)} %rest_0_.1, f32[4]{0:T(128)} %rest_1_.1, f32[4]{0:T(128)} %rest_2_.1, f32[3,4]{1,0:T(4,128)} %rest_3_.1, f32[3]{0:T(128)} %rest_4_.1), custom_call_target="tpu_custom_call" | custom-call | tf_op jit(solution)/shard_map/raycast/pallas_call | solution.py:527
  27.7 1.6 %copy.8 = f32[4,64,64]{2,1,0:T(8,128)} copy(f32[4,64,64]{2,1,0:T(8,128)} %raycast.1) | data formatting | bytes 131072

commit v2 on v1

--- a/solution.py
+++ b/solution.py
@@ -13,8 +13,9 @@
 SUB = 8
 LAG = 8
 WIDE = 2
-DRAIN = 2
-EARLY = 16
+DRAIN = 4
+RATE = 2
+EARLY = 22
 LOG2E = math.log2(math.e)
 POWER = 8
 RANGE = 11.0
@@ -155,15 +156,15 @@
             + n // 2
         )
         pl.semaphore_wait(barrier, expected)
-        for side in range(2):
-            @pl.when(has_target[side])
-            def _(side=side):
-                def send(i, carry):
+        def send(i, carry):
+            for side in range(2):
+                @pl.when(has_target[side])
+                def _(side=side):
                     z_copy(band_of(i), side).start()
-                    return carry
-
-                lax.fori_loop(0, bands, send, 0)
-
+
+            return carry
+
+        lax.fori_loop(0, bands, send, 0)
         for side in range(2):
             @pl.when(row_target[side])
             def _(side=side):
@@ -233,6 +234,7 @@
                 def _(side=side):
                     z_copy(b, side).wait_recv()
 
+    def wait_rows(s):
         @pl.when(s == max(bands - 2, 0) * tiles)
         def _():
             for side in range(2):
@@ -384,12 +386,16 @@
             def _(i=i):
                 own_copy(s, i).start()
 
-    early = min(EARLY, tiles * max(bands - 2, 0))
-    early = early - early % (2 * WIDE)
-    late = early // 2 if early else min(LAG, units)
-    turn = early + late
+    early = min(EARLY, units) if bands > 2 else 0
+    early = early - early % WIDE
+    catch = min(early // RATE, units - early) if early else min(LAG, units)
+    turn = early + catch
+    late = turn - RATE * catch if early else catch
+    edge = max(bands - 2, 0) * tiles
 
     def inner(s, carry):
+        if edge < early:
+            wait_rows(s)
         shade(s, True, False)
         return carry
 
@@ -397,6 +403,9 @@
         @pl.when(jnp.logical_and(lax.rem(s, tiles) == 0, s > 0))
         def _():
             wait_halos(s)
+
+        if edge >= early:
+            wait_rows(s)
 
     def outer(i, carry):
         first = i * WIDE
@@ -443,10 +452,10 @@
     lax.fori_loop(0, early // WIDE, outer, 0)
     if early:
         lax.fori_loop(
-            early, turn, step_with(lambda s: [2 * (s - early), 2 * (s - early) + 1]), 0
+            early, turn, step_with(lambda s: [RATE * (s - early) + r for r in range(RATE)]), 0
         )
     else:
-        lax.fori_loop(0, late, step_with(lambda s: []), 0)
+        lax.fori_loop(0, turn, step_with(lambda s: []), 0)
     lax.fori_loop(turn, units, step_with(lambda s: [s - late]), 0)
     width = DRAIN if late % DRAIN == 0 else 1
     lax.fori_loop(0, late // width, drain_from(units - late, width), 0)

time: 29.4 us -> 28.1 us (0.956)
  Pallas kernels: 27.7 us -> 26.4 us
    pallas_call x1, Pallas kernels: 27.7 us -> 26.4 us  [shards(): pl.pallas_call(functools.partial(kernel, n, m), out_shape=jax.ShapeDtypeS...]
where the time goes in v2:
time: 28.1 us; the launch traced here: 27.9 us
  Pallas kernels  26.4 us (94%)
  local copies, waits for them, and re-layouts  1.57 us (6%)
    pallas_call x1, Pallas kernels, shards(): pl.pallas_call(functools.partial(kernel, n, m), out_shape=jax.ShapeDtypeS...  26.4 us
    unnamed x1, local copies, waits for them, and re-layouts  1.57 us

profile of v2, /device:TPU:0, one launch (start us, length us, event | category | flops | bytes accessed | tf_op | source)
XLA Modules:
  0.0 27.9 jit_solution(8535045025953709281)
XLA Ops:
  0.0 26.4 %raycast.1 = f32[4,64,64]{2,1,0:T(8,128)} custom-call(bf16[16,64,1024]{2,1,0:T(8,128)(2,1)} %field.1, f32[4]{0:T(128)} %rest_0_.1, f32[4]{0:T(128)} %rest_1_.1, f32[4]{0:T(128)} %rest_2_.1, f32[3,4]{1,0:T(4,128)} %rest_3_.1, f32[3]{0:T(128)} %rest_4_.1), custom_call_target="tpu_custom_call" | custom-call | tf_op jit(solution)/shard_map/raycast/pallas_call | solution.py:536
  26.4 1.6 %copy.8 = f32[4,64,64]{2,1,0:T(8,128)} copy(f32[4,64,64]{2,1,0:T(8,128)} %raycast.1) | data formatting | bytes 131072
